TPU v7x, 32 devices: a whole 2x2x4 slice. The times are simulated.
32 devices in a mesh: chan: 8 (over z, core), rad: 4 (over y, x).
Axes of the slice: x: 2, y: 2, z: 4, core: 2. Of those that a mesh axis runs over, the one named last changes fastest.
Arguments:
- wave_field: float32 [2, 128, 32, 1024], P(None, 'chan', 'rad'), may hold values from -6 to 6
- partner: int32 [128, 8], replicated, may hold values from 0 to 127, as said below
- coupling_kind: int32 [128, 8], replicated, may hold values from 0 to 3
- coupling: float32 [128, 8], replicated, may hold values from -1 to 1
- angular: int32 [128, 2], replicated, may hold values from 0 to 11
Outputs:
- advanced: float32 [2, 128, 32, 1024], P(None, 'chan', 'rad')
Inputs may be any that keep to these rules, and one draw needn't show every extreme that they name: partner[c, s] differs from c by at most 8; entry 0 of every channel lies exactly 8 away and entry 1 is the channel itself.
All inputs are finite; a program needn't handle non-finite values.
Results may differ from a plain program's by a relative error of at most 0.0003.
Values sent between devices are 32-bit elements; how exact they have to be, the bound alone decides.
A program may use at most 64 MiB of HBM per device.

v0:
```python
import functools

import jax
import jax.numpy as jnp
from jax import lax
from jax.experimental import pallas as pl
from jax.experimental.pallas import tpu as pltpu
from jax.sharding import PartitionSpec as P

KINDS = 4
ELL_BASE = 64

time_step = 0.004
grid_step = 0.2
radius_start = 1.0
kinetic_scale = -1.0 / (24.0 * grid_step * grid_step)

RIGHT, LEFT, DOWN, UP, DOWN_HI, UP_HI, RELAY, FORWARD = range(8)


def kernel(
    word_ref, coef_ref, wave_ref, out_ref,
    words, coefs, forms,
    ext_w0, ext_w1, ext_f1, ext_f0, base_a, base_b, pack, above, below, relay, out_buf,
    table_sem, local_sem, out_sem, send_sem, recv_sem,
):
    nchan, nrows, ncols = wave_ref.shape[1:]
    nentries = coef_ref.shape[0]
    reach = nchan // 2
    group = nrows // 2
    chan, rad = lax.axis_index("chan"), lax.axis_index("rad")
    chans, rads = lax.axis_size("chan"), lax.axis_size("rad")
    chan_start = chan * nchan
    has = {RIGHT: chan < chans - 1, LEFT: chan > 0, DOWN: rad < rads - 1, UP: rad > 0}
    target = {
        RIGHT: {"chan": chan + 1}, LEFT: {"chan": chan - 1},
        DOWN: {"rad": rad + 1}, UP: {"rad": rad - 1},
    }
    opposite = {RIGHT: LEFT, LEFT: RIGHT, DOWN: UP, UP: DOWN}
    own = pl.ds(reach, nchan)
    exts = (ext_w0, ext_w1, ext_f1, ext_f0)

    barrier = pltpu.get_barrier_semaphore()
    for way in range(4):
        @pl.when(has[way])
        def _():
            pl.semaphore_signal(
                barrier, inc=1, device_id=target[way], device_id_type=pl.DeviceIdType.MESH
            )
    relayed = rads == 4
    across = {"rad": lax.rem(rad + 2, rads)}
    if relayed:
        pl.semaphore_signal(barrier, inc=1, device_id=across, device_id_type=pl.DeviceIdType.MESH)

    fills = [
        pltpu.make_async_copy(wave_ref.at[p], exts[p].at[own], local_sem.at[p]) for p in range(2)
    ]
    tables = [
        pltpu.make_async_copy(src, dst, table_sem.at[i])
        for i, (src, dst) in enumerate(
            ((word_ref, words), (coef_ref, coefs))
        )
    ]
    for copy in fills + tables:
        copy.start()

    def remote(source, dest, phase, sent, received, device):
        return pltpu.make_async_remote_copy(
            src_ref=source, dst_ref=dest,
            send_sem=send_sem.at[phase, sent], recv_sem=recv_sem.at[phase, received],
            device_id=device, device_id_type=pl.DeviceIdType.MESH,
        )

    half = nchan // group // 2
    low, high = pl.ds(0, half), pl.ds(half, half)

    def copy_of(phase, way):
        ext = exts[phase]
        if way == RIGHT:
            source = wave_ref.at[phase, pl.ds(reach, reach)] if phase < 2 else ext.at[pl.ds(nchan, reach)]
            dest = ext.at[pl.ds(0, reach)]
        elif way == LEFT:
            source = wave_ref.at[phase, pl.ds(0, reach)] if phase < 2 else ext.at[pl.ds(reach, reach)]
            dest = ext.at[pl.ds(reach + nchan, reach)]
        elif way == DOWN:
            source, dest = pack.at[phase, 0, low], above.at[phase, low]
        elif way == UP:
            source, dest = pack.at[phase, 1, low], below.at[phase, low]
        elif way == DOWN_HI:
            source, dest = pack.at[phase, 0, high], above.at[phase, high]
        else:
            source, dest = pack.at[phase, 1, high], below.at[phase, high]
        toward = {DOWN_HI: DOWN, UP_HI: UP}.get(way, way)
        return remote(source, dest, phase, way, way, target[toward])

    def to_relay(phase, way):
        side = 0 if way == DOWN_HI else 1
        return remote(pack.at[phase, side, high], relay.at[phase], phase, way, RELAY, across)

    middle = {DOWN_HI: rad == 1, UP_HI: rad == 2}

    def send_one(phase, way):
        if way in middle:
            direct = has[DOWN if way == DOWN_HI else UP]
            if relayed:
                direct = jnp.logical_and(direct, jnp.logical_not(middle[way]))

                @pl.when(middle[way])
                def _():
                    to_relay(phase, way).start()
        else:
            direct = has[way]

        @pl.when(direct)
        def _():
            copy_of(phase, way).start()

    def send_rows(phase):
        for way in (DOWN, UP, DOWN_HI, UP_HI):
            send_one(phase, way)

    def send_channels(phase):
        for way in (RIGHT, LEFT):
            send_one(phase, way)

    def forward(phase):
        if relayed:
            @pl.when(rad == 3)
            def _():
                to_relay(phase, DOWN_HI).wait_recv()
                remote(relay.at[phase], above.at[phase, high], phase, FORWARD, DOWN_HI, target[UP]).start()

            @pl.when(rad == 0)
            def _():
                to_relay(phase, UP_HI).wait_recv()
                remote(relay.at[phase], below.at[phase, high], phase, FORWARD, UP_HI, target[DOWN]).start()

    def receive_channels(phase):
        for way in (RIGHT, LEFT):
            @pl.when(has[opposite[way]])
            def _():
                copy_of(phase, way).wait_recv()

    def receive_rows(phase):
        for way, other in ((DOWN, UP), (UP, DOWN), (DOWN_HI, UP), (UP_HI, DOWN)):
            @pl.when(has[other])
            def _():
                copy_of(phase, way).wait_recv()

    def wait_sent(phase):
        for way, needs in ((RIGHT, RIGHT), (LEFT, LEFT), (DOWN, DOWN), (UP, UP), (DOWN_HI, DOWN), (UP_HI, UP)):
            @pl.when(has[needs])
            def _():
                copy_of(phase, way).wait_send()
        if relayed:
            @pl.when(jnp.logical_or(rad == 0, rad == 3))
            def _():
                remote(relay.at[phase], above.at[phase, high], phase, FORWARD, DOWN_HI, across).wait_send()

    row = lax.broadcasted_iota(jnp.int32, (nrows, ncols), 0)
    col = lax.broadcasted_iota(jnp.int32, (nrows, ncols), 1)
    radius_one = radius_start + grid_step * (rad * nrows + row).astype(jnp.float32)
    radius_two = radius_start + grid_step * col.astype(jnp.float32)
    greater = jnp.maximum(radius_one, radius_two)
    lesser = jnp.minimum(radius_one, radius_two)
    forms[0] = radius_one
    forms[1] = radius_two
    forms[2] = 1.0 / greater
    forms[3] = lesser / (greater * greater)
    forms[4] = 0.5 / (radius_one * radius_one)
    forms[5] = 0.5 / (radius_two * radius_two)

    for edge, way in ((above, UP), (below, DOWN)):
        @pl.when(jnp.logical_not(has[way]))
        def _():
            edge[...] = jnp.zeros_like(edge)

    def turn(value, amount, axis=0):
        amount %= value.shape[axis]
        return pltpu.roll(value, amount, axis) if amount else value

    def packed(value, side, k, tile):
        value = value * kinetic_scale
        if side == 0:
            rows = jnp.where(row == nrows - 2, 16.0 * turn(value, -1) - value, -value)
            rows = turn(rows, 2 * k + 2)
        else:
            rows = jnp.where(row == 1, 16.0 * turn(value, 1) - value, -value)
            rows = turn(rows, 2 * k)
        return rows if tile is None else jnp.where(row < 2 * k, tile, rows)

    def pack_rows(phase):
        ext = exts[phase]

        def step(q, carry):
            for side in range(2):
                tile = None
                for k in range(group):
                    tile = packed(ext[reach + q * group + k], side, k, tile)
                pack[phase, side, q] = tile
            return carry

        lax.fori_loop(0, nchan // group, step, 0)

    def local_part(phase, base):
        ext = exts[phase]

        def step(c, carry):
            value = ext[reach + c]
            one = lax.div(words[nentries, chan_start + c], ELL_BASE).astype(jnp.float32)
            two = lax.rem(words[nentries, chan_start + c], ELL_BASE).astype(jnp.float32)
            near = jnp.where(col >= 1, turn(value, 1, 1), 0.0) + jnp.where(col < ncols - 1, turn(value, -1, 1), 0.0)
            near += jnp.where(row >= 1, turn(value, 1), 0.0) + jnp.where(row < nrows - 1, turn(value, -1), 0.0)
            far = jnp.where(col >= 2, turn(value, 2, 1), 0.0) + jnp.where(col < ncols - 2, turn(value, -2, 1), 0.0)
            far += jnp.where(row >= 2, turn(value, 2), 0.0) + jnp.where(row < nrows - 2, turn(value, -2), 0.0)
            kinetic = (16.0 * near - far - 60.0 * value) * kinetic_scale
            diagonal = (one * (one + 1.0)) * forms[4] + (two * (two + 1.0)) * forms[5]
            base[c] = kinetic + diagonal * value
            return carry

        lax.fori_loop(0, nchan, step, 0, unroll=group * 2)

    def coupled_part(phase, base):
        ext = exts[phase]

        def step(c, carry):
            total = base[c]
            for s in range(nentries):
                word = words[s, chan_start + c]
                link = lax.div(word, KINDS) - chan_start + reach
                picked = ext[jnp.clip(link, 0, nchan + 2 * reach - 1)]
                weight = coefs[s, chan_start + c] * forms[lax.rem(word, KINDS)]
                total += weight * picked
            base[c] = total
            return carry

        lax.fori_loop(0, nchan, step, 0, unroll=group * 2)

    def edge_part(phase, base, emit, packs=None):
        def step(q, carry):
            upper, lower = above[phase, q], below[phase, q]
            tiles = [None, None]
            for k in range(group):
                c = q * group + k
                edge = jnp.where(row < nrows // 2, turn(upper, -2 * k), turn(lower, nrows - 2 - 2 * k))
                edge = jnp.where((row < 2) | (row >= nrows - 2), edge, 0.0)
                value = emit(c, base[c] + edge)
                if packs is not None:
                    tiles = [packed(value, side, k, tiles[side]) for side in range(2)]
            if packs is not None:
                for side in range(2):
                    pack[packs, side, q] = tiles[side]
            return carry

        lax.fori_loop(0, nchan // group, step, 0)

    fills[0].wait()
    pack_rows(0)
    neighbours = sum(has[way].astype(jnp.int32) for way in range(4)) + int(relayed)
    pl.semaphore_wait(barrier, neighbours)
    send_rows(0)
    send_channels(0)
    for copy in tables:
        copy.wait()

    def emit_f1(c, total):
        value = -time_step * total
        ext_f1[reach + c] = value
        return value

    def emit_f0(c, total):
        value = time_step * total
        ext_f0[reach + c] = value
        return value

    def emit_out0(c, total):
        out_buf[0, c] = ext_w0[reach + c] + ext_f0[reach + c] + (0.5 * time_step) * total

    def emit_out1(c, total):
        out_buf[1, c] = ext_w1[reach + c] + ext_f1[reach + c] - (0.5 * time_step) * total

    local_part(0, base_a)
    fills[1].wait()
    pack_rows(1)
    local_part(1, base_b)
    forward(0)
    send_rows(1)
    send_channels(1)
    receive_channels(0)
    coupled_part(0, base_a)
    forward(1)
    receive_rows(0)
    edge_part(0, base_a, emit_f1, 2)
    send_rows(2)
    send_channels(2)
    local_part(2, base_a)
    receive_channels(1)
    coupled_part(1, base_b)
    forward(2)
    receive_rows(1)
    edge_part(1, base_b, emit_f0, 3)
    send_rows(3)
    send_channels(3)
    local_part(3, base_b)
    receive_channels(2)
    coupled_part(2, base_a)
    forward(3)
    receive_rows(2)
    edge_part(2, base_a, emit_out0)
    stores = [pltpu.make_async_copy(out_buf.at[p], out_ref.at[p], out_sem.at[p]) for p in range(2)]
    stores[0].start()
    receive_channels(3)
    coupled_part(3, base_b)
    receive_rows(3)
    edge_part(3, base_b, emit_out1)
    stores[1].start()
    for phase in range(4):
        wait_sent(phase)
    for copy in stores:
        copy.wait()


def body(wave_field, partner, coupling_kind, coupling, angular):
    parts, nchan, nrows, ncols = wave_field.shape
    words = jnp.concatenate(
        [partner.T * KINDS + coupling_kind.T, (angular[:, 0] * ELL_BASE + angular[:, 1])[None]]
    )
    tables = (words, coupling.T)
    reach = nchan // 2
    group = nrows // 2
    tiles = nchan // group
    f32 = jnp.float32
    ext = pltpu.VMEM((nchan + 2 * reach, nrows, ncols), f32)
    base = pltpu.VMEM((nchan, nrows, ncols), f32)
    anywhere = pl.BlockSpec(memory_space=pl.ANY)
    return pl.pallas_call(
        kernel,
        out_shape=jax.ShapeDtypeStruct(wave_field.shape, f32),
        in_specs=[anywhere] * 2 + [pl.BlockSpec(memory_space=pltpu.HBM)],
        out_specs=anywhere,
        scratch_shapes=[
            *(pltpu.SMEM(table.shape, table.dtype) for table in tables),
            pltpu.VMEM((KINDS + 2, nrows, ncols), f32),
            ext, ext, ext, ext, base, base,
            pltpu.VMEM((4, 2, tiles, nrows, ncols), f32),
            pltpu.VMEM((4, tiles, nrows, ncols), f32),
            pltpu.VMEM((4, tiles, nrows, ncols), f32),
            pltpu.VMEM((4, tiles // 2, nrows, ncols), f32),
            pltpu.VMEM((parts, nchan, nrows, ncols), f32),
            pltpu.SemaphoreType.DMA((2,)),
            pltpu.SemaphoreType.DMA((2,)),
            pltpu.SemaphoreType.DMA((2,)),
            pltpu.SemaphoreType.DMA((4, 8)),
            pltpu.SemaphoreType.DMA((4, 8)),
        ],
        compiler_params=pltpu.CompilerParams(
            collective_id=0, has_side_effects=True, vmem_limit_bytes=52 * 2**20
        ),
        name="taylor_step",
    )(*tables, wave_field)


def solution(mesh):
    placed = (P(None, "chan", "rad", None), P(), P(), P(), P())
    return jax.shard_map(
        body, mesh=mesh, in_specs=placed, out_specs=P(None, "chan", "rad", None), check_vma=False
    )
```

profile of v0, /device:TPU:0, one launch (start us, length us, event | category | flops | bytes accessed | tf_op | source)
XLA Modules:
  0.0 26.3 jit_solution(14725700979569399499)
XLA Ops:
  0.0 0.0 copy-start.1
  0.0 0.7 %copy-done.1 = s32[128,2]{0,1:T(2,128)S(1)} copy-done((s32[128,2]{0,1:T(2,128)S(1)}, s32[128,2]{0,1:T(2,128)}, u32[]{:S(2)}) %copy-start.1) | copy-done | bytes 1048
  0.7 0.7 %add_bitcast_fusion = s32[8,128]{1,0:T(8,128)S(1)} fusion(s32[128,8]{0,1:T(8,128)} %param.7, s32[128,8]{0,1:T(8,128)} %param.6), kind=kLoop, calls=%fused_computation.1 | loop fusion | flops 2048 | bytes 12288 | tf_op jit(solution)/shard_map/add | solution.py:326
  1.4 0.0 copy-start
  1.4 0.7 %copy-done = f32[128,8]{0,1:T(8,128)S(1)} copy-done((f32[128,8]{0,1:T(8,128)S(1)}, f32[128,8]{0,1:T(8,128)}, u32[]{:S(2)}) %copy-start) | copy-done | bytes 4120
  2.1 23.2 %taylor_step.1 = f32[2,16,8,1024]{3,2,1,0:T(8,128)S(1)} custom-call(s32[9,128]{1,0:T(8,128)S(1)} %pad_add_fusion.word_ref, f32[8,128]{1,0:T(8,128)S(1)} %bitcast.5, f32[2,16,8,1024]{3,2,1,0:T(8,128)} %wave_ref.1), custom_call_target="tpu_custom_call" | custom-call | tf_op jit(solution)/shard_map/taylor_step/pallas_call | solution.py:336
  25.3 1.0 %copy.7 = f32[2,16,8,1024]{3,2,1,0:T(8,128)} copy(f32[2,16,8,1024]{3,2,1,0:T(8,128)S(1)} %taylor_step.1) | data formatting | bytes 2097152
  (2 shorter events, 0.0 us)
Async XLA Ops:
  0.0 0.7 %copy-start.1 = (s32[128,2]{0,1:T(2,128)S(1)}, s32[128,2]{0,1:T(2,128)}, u32[]{:S(2)}) copy-start(s32[128,2]{0,1:T(2,128)} %param.9) | copy-start | bytes 3076
  1.4 0.7 %copy-start = (f32[128,8]{0,1:T(8,128)S(1)}, f32[128,8]{0,1:T(8,128)}, u32[]{:S(2)}) copy-start(f32[128,8]{0,1:T(8,128)} %param.8) | copy-start | bytes 12292
where the time goes:
time: 26.5 us; the launch traced here: 26.3 us
  Pallas kernels  23.2 us (88%)
  local copies, waits for them, and re-layouts  2.33 us (9%)
  other arithmetic  0.72 us (3%)
    pallas_call x1, Pallas kernels, body(): pl.pallas_call(kernel, out_shape=jax.ShapeDtypeStruct(wave_field.shape, f...  23.2 us
    unnamed x5, local copies, waits for them, and re-layouts  2.33 us
    add x1, other arithmetic, body(): partner.T * KINDS + coupling_kind.T  0.71 us

commit v1 on v0

--- a/solution.py
+++ b/solution.py
@@ -8,7 +8,6 @@
 from jax.sharding import PartitionSpec as P
 
 KINDS = 4
-ELL_BASE = 64
 
 time_step = 0.004
 grid_step = 0.2
@@ -19,10 +18,10 @@
 
 
 def kernel(
-    word_ref, coef_ref, wave_ref, out_ref,
-    words, coefs, forms,
-    ext_w0, ext_w1, ext_f1, ext_f0, base_a, base_b, pack, above, below, relay, out_buf,
-    table_sem, local_sem, out_sem, send_sem, recv_sem,
+    partner_ref, kind_ref, coef_ref, angular_ref, wave_ref, out_ref,
+    links, kinds, coefs, angulars, forms,
+    ext_w0, ext_w1, ext_f1, ext_f0, base_a, base_b, pack, above, below, relay,
+    table_sem, local_sem, send_sem, recv_sem,
 ):
     nchan, nrows, ncols = wave_ref.shape[1:]
     nentries = coef_ref.shape[0]
@@ -58,7 +57,7 @@
     tables = [
         pltpu.make_async_copy(src, dst, table_sem.at[i])
         for i, (src, dst) in enumerate(
-            ((word_ref, words), (coef_ref, coefs))
+            ((partner_ref, links), (kind_ref, kinds), (coef_ref, coefs), (angular_ref, angulars))
         )
     ]
     for copy in fills + tables:
@@ -207,8 +206,8 @@
 
         def step(c, carry):
             value = ext[reach + c]
-            one = lax.div(words[nentries, chan_start + c], ELL_BASE).astype(jnp.float32)
-            two = lax.rem(words[nentries, chan_start + c], ELL_BASE).astype(jnp.float32)
+            one = angulars[0, chan_start + c].astype(jnp.float32)
+            two = angulars[1, chan_start + c].astype(jnp.float32)
             near = jnp.where(col >= 1, turn(value, 1, 1), 0.0) + jnp.where(col < ncols - 1, turn(value, -1, 1), 0.0)
             near += jnp.where(row >= 1, turn(value, 1), 0.0) + jnp.where(row < nrows - 1, turn(value, -1), 0.0)
             far = jnp.where(col >= 2, turn(value, 2, 1), 0.0) + jnp.where(col < ncols - 2, turn(value, -2, 1), 0.0)
@@ -226,10 +225,9 @@
         def step(c, carry):
             total = base[c]
             for s in range(nentries):
-                word = words[s, chan_start + c]
-                link = lax.div(word, KINDS) - chan_start + reach
+                link = links[s, chan_start + c] - chan_start + reach
                 picked = ext[jnp.clip(link, 0, nchan + 2 * reach - 1)]
-                weight = coefs[s, chan_start + c] * forms[lax.rem(word, KINDS)]
+                weight = coefs[s, chan_start + c] * forms[kinds[s, chan_start + c]]
                 total += weight * picked
             base[c] = total
             return carry
@@ -274,10 +272,10 @@
         return value
 
     def emit_out0(c, total):
-        out_buf[0, c] = ext_w0[reach + c] + ext_f0[reach + c] + (0.5 * time_step) * total
+        out_ref[0, c] = ext_w0[reach + c] + ext_f0[reach + c] + (0.5 * time_step) * total
 
     def emit_out1(c, total):
-        out_buf[1, c] = ext_w1[reach + c] + ext_f1[reach + c] - (0.5 * time_step) * total
+        out_ref[1, c] = ext_w1[reach + c] + ext_f1[reach + c] - (0.5 * time_step) * total
 
     local_part(0, base_a)
     fills[1].wait()
@@ -307,37 +305,28 @@
     forward(3)
     receive_rows(2)
     edge_part(2, base_a, emit_out0)
-    stores = [pltpu.make_async_copy(out_buf.at[p], out_ref.at[p], out_sem.at[p]) for p in range(2)]
-    stores[0].start()
     receive_channels(3)
     coupled_part(3, base_b)
     receive_rows(3)
     edge_part(3, base_b, emit_out1)
-    stores[1].start()
     for phase in range(4):
         wait_sent(phase)
-    for copy in stores:
-        copy.wait()
 
 
 def body(wave_field, partner, coupling_kind, coupling, angular):
     parts, nchan, nrows, ncols = wave_field.shape
-    words = jnp.concatenate(
-        [partner.T * KINDS + coupling_kind.T, (angular[:, 0] * ELL_BASE + angular[:, 1])[None]]
-    )
-    tables = (words, coupling.T)
+    tables = (partner.T, coupling_kind.T, coupling.T, angular.T)
     reach = nchan // 2
     group = nrows // 2
     tiles = nchan // group
     f32 = jnp.float32
     ext = pltpu.VMEM((nchan + 2 * reach, nrows, ncols), f32)
     base = pltpu.VMEM((nchan, nrows, ncols), f32)
-    anywhere = pl.BlockSpec(memory_space=pl.ANY)
     return pl.pallas_call(
         kernel,
-        out_shape=jax.ShapeDtypeStruct(wave_field.shape, f32),
-        in_specs=[anywhere] * 2 + [pl.BlockSpec(memory_space=pltpu.HBM)],
-        out_specs=anywhere,
+        out_shape=pltpu.VMEM(wave_field.shape, f32),
+        in_specs=[pl.BlockSpec(memory_space=pltpu.HBM)] * 5,
+        out_specs=pl.BlockSpec(memory_space=pltpu.VMEM),
         scratch_shapes=[
             *(pltpu.SMEM(table.shape, table.dtype) for table in tables),
             pltpu.VMEM((KINDS + 2, nrows, ncols), f32),
@@ -346,15 +335,13 @@
             pltpu.VMEM((4, tiles, nrows, ncols), f32),
             pltpu.VMEM((4, tiles, nrows, ncols), f32),
             pltpu.VMEM((4, tiles // 2, nrows, ncols), f32),
-            pltpu.VMEM((parts, nchan, nrows, ncols), f32),
-            pltpu.SemaphoreType.DMA((2,)),
-            pltpu.SemaphoreType.DMA((2,)),
+            pltpu.SemaphoreType.DMA((4,)),
             pltpu.SemaphoreType.DMA((2,)),
             pltpu.SemaphoreType.DMA((4, 8)),
             pltpu.SemaphoreType.DMA((4, 8)),
         ],
         compiler_params=pltpu.CompilerParams(
-            collective_id=0, has_side_effects=True, vmem_limit_bytes=52 * 2**20
+            collective_id=0, has_side_effects=True, vmem_limit_bytes=67_043_328 - 4 * wave_field.size
         ),
         name="taylor_step",
     )(*tables, wave_field)

time: 26.5 us -> 24.3 us (0.917)
  local copies, waits for them, and re-layouts: 2.33 us -> 0.97 us
  other arithmetic: 0.72 us -> 0 us
    unnamed x5 -> x1, local copies, waits for them, and re-layouts: 2.33 us -> 0.97 us
    add x2 -> x0, other arithmetic: 0.71 us -> none  [the longest x1 0.71 us: body(): partner.T * KINDS + coupling_kind.T]
where the time goes in v1:
time: 24.3 us; the launch traced here: 24.1 us
  Pallas kernels  23.2 us (95%)
  local copies, waits for them, and re-layouts  0.97 us (4%)
    pallas_call x1, Pallas kernels, body(): pl.pallas_call(kernel, out_shape=pltpu.VMEM(wave_field.shape, f32), in_sp...  23.2 us
    unnamed x1, local copies, waits for them, and re-layouts  0.97 us

profile of v1, /device:TPU:0, one launch (start us, length us, event | category | flops | bytes accessed | tf_op | source)
XLA Modules:
  0.0 24.1 jit_solution(923742535249644426)
XLA Ops:
  0.0 23.2 %taylor_step.1 = f32[2,16,8,1024]{3,2,1,0:T(8,128)S(1)} custom-call(s32[8,128]{1,0:T(8,128)} %bitcast.4, s32[8,128]{1,0:T(8,128)} %bitcast.5, f32[8,128]{1,0:T(8,128)} %bitcast.6, s32[2,128]{1,0:T(2,128)} %bitcast.7, f32[2,16,8,1024]{3,2,1,0:T(8,128)} %wave_ref.1), custom_call_target="tpu_custom_call" | custom-call | tf_op jit(solution)/shard_map/taylor_step/pallas_call | solution.py:325
  23.2 1.0 %copy.7 = f32[2,16,8,1024]{3,2,1,0:T(8,128)} copy(f32[2,16,8,1024]{3,2,1,0:T(8,128)S(1)} %taylor_step.1) | data formatting | bytes 2097152

commit v2 on v1

--- a/solution.py
+++ b/solution.py
@@ -14,14 +14,15 @@
 radius_start = 1.0
 kinetic_scale = -1.0 / (24.0 * grid_step * grid_step)
 
-RIGHT, LEFT, DOWN, UP, DOWN_HI, UP_HI, RELAY, FORWARD = range(8)
+RIGHT, LEFT, DOWN, UP, DOWN_HI, UP_HI = range(6)
+FORWARD = DOWN_HI
 
 
 def kernel(
     partner_ref, kind_ref, coef_ref, angular_ref, wave_ref, out_ref,
     links, kinds, coefs, angulars, forms,
     ext_w0, ext_w1, ext_f1, ext_f0, base_a, base_b, pack, above, below, relay,
-    table_sem, local_sem, send_sem, recv_sem,
+    table_sem, local_sem, send_sem, recv_sem, met_sem,
 ):
     nchan, nrows, ncols = wave_ref.shape[1:]
     nentries = coef_ref.shape[0]
@@ -39,15 +40,21 @@
     own = pl.ds(reach, nchan)
     exts = (ext_w0, ext_w1, ext_f1, ext_f0)
 
+    relayed = rads == 4
+    ends, mids = jnp.logical_or(rad == 0, rad == 3), jnp.logical_or(rad == 1, rad == 2)
+    across = {"rad": lax.rem(rad + 2, rads)}
+    meets = dict(has)
+    if relayed:
+        meets[DOWN] = jnp.logical_or(rad == 0, rad == 2)
+        meets[UP] = jnp.logical_or(rad == 1, rad == 3)
+
     barrier = pltpu.get_barrier_semaphore()
     for way in range(4):
-        @pl.when(has[way])
+        @pl.when(meets[way])
         def _():
             pl.semaphore_signal(
                 barrier, inc=1, device_id=target[way], device_id_type=pl.DeviceIdType.MESH
             )
-    relayed = rads == 4
-    across = {"rad": lax.rem(rad + 2, rads)}
     if relayed:
         pl.semaphore_signal(barrier, inc=1, device_id=across, device_id_type=pl.DeviceIdType.MESH)
 
@@ -66,61 +73,54 @@
     def remote(source, dest, phase, sent, received, device):
         return pltpu.make_async_remote_copy(
             src_ref=source, dst_ref=dest,
-            send_sem=send_sem.at[phase, sent], recv_sem=recv_sem.at[phase, received],
+            send_sem=send_sem.at[sent], recv_sem=recv_sem.at[phase, received],
             device_id=device, device_id_type=pl.DeviceIdType.MESH,
         )
 
-    half = nchan // group // 2
+    tiles = nchan // group
+    half = tiles // 2
     low, high = pl.ds(0, half), pl.ds(half, half)
+    halves = ((0, half), (half, tiles))
+    lines = ((DOWN, UP), (DOWN_HI, UP_HI))
 
     def copy_of(phase, way):
         ext = exts[phase]
         if way == RIGHT:
             source = wave_ref.at[phase, pl.ds(reach, reach)] if phase < 2 else ext.at[pl.ds(nchan, reach)]
-            dest = ext.at[pl.ds(0, reach)]
-        elif way == LEFT:
+            return remote(source, ext.at[pl.ds(0, reach)], phase, way, way, target[way])
+        if way == LEFT:
             source = wave_ref.at[phase, pl.ds(0, reach)] if phase < 2 else ext.at[pl.ds(reach, reach)]
-            dest = ext.at[pl.ds(reach + nchan, reach)]
-        elif way == DOWN:
-            source, dest = pack.at[phase, 0, low], above.at[phase, low]
-        elif way == UP:
-            source, dest = pack.at[phase, 1, low], below.at[phase, low]
-        elif way == DOWN_HI:
-            source, dest = pack.at[phase, 0, high], above.at[phase, high]
-        else:
-            source, dest = pack.at[phase, 1, high], below.at[phase, high]
-        toward = {DOWN_HI: DOWN, UP_HI: UP}.get(way, way)
-        return remote(source, dest, phase, way, way, target[toward])
+            return remote(source, ext.at[pl.ds(reach + nchan, reach)], phase, way, way, target[way])
+        down = way in (DOWN, DOWN_HI)
+        part = low if way in (DOWN, UP) else high
+        edge = above if down else below
+        toward = DOWN if down else UP
+        return remote(pack.at[1 - down, phase, part], edge.at[phase, part], phase, toward, way, target[toward])
 
     def to_relay(phase, way):
-        side = 0 if way == DOWN_HI else 1
-        return remote(pack.at[phase, side, high], relay.at[phase], phase, way, RELAY, across)
-
-    middle = {DOWN_HI: rad == 1, UP_HI: rad == 2}
-
-    def send_one(phase, way):
-        if way in middle:
-            direct = has[DOWN if way == DOWN_HI else UP]
-            if relayed:
-                direct = jnp.logical_and(direct, jnp.logical_not(middle[way]))
-
-                @pl.when(middle[way])
-                def _():
-                    to_relay(phase, way).start()
-        else:
-            direct = has[way]
-
-        @pl.when(direct)
+        side, received = (0, UP_HI) if way == DOWN_HI else (1, DOWN_HI)
+        return remote(pack.at[side, phase, high], relay.at[phase], phase, (DOWN, UP)[side], received, across)
+
+    def send_far(phase, part):
+        if relayed:
+            @pl.when(rad == 1)
+            def _():
+                copy_of(phase, DOWN).start() if part == 0 else to_relay(phase, DOWN_HI).start()
+
+            @pl.when(rad == 2)
+            def _():
+                copy_of(phase, UP).start() if part == 0 else to_relay(phase, UP_HI).start()
+
+    def send_near(phase, part):
+        for way, toward in zip(lines[part], (DOWN, UP)):
+            @pl.when(meets[toward])
+            def _():
+                copy_of(phase, way).start()
+
+    def send_channel(phase, way):
+        @pl.when(has[way])
         def _():
             copy_of(phase, way).start()
-
-    def send_rows(phase):
-        for way in (DOWN, UP, DOWN_HI, UP_HI):
-            send_one(phase, way)
-
-    def send_channels(phase):
-        for way in (RIGHT, LEFT):
-            send_one(phase, way)
 
     def forward(phase):
         if relayed:
@@ -140,21 +140,24 @@
             def _():
                 copy_of(phase, way).wait_recv()
 
-    def receive_rows(phase):
-        for way, other in ((DOWN, UP), (UP, DOWN), (DOWN_HI, UP), (UP_HI, DOWN)):
+    def receive_rows(phase, part):
+        for way, other in zip(lines[part], (UP, DOWN)):
             @pl.when(has[other])
             def _():
                 copy_of(phase, way).wait_recv()
 
-    def wait_sent(phase):
-        for way, needs in ((RIGHT, RIGHT), (LEFT, LEFT), (DOWN, DOWN), (UP, UP), (DOWN_HI, DOWN), (UP_HI, UP)):
-            @pl.when(has[needs])
-            def _():
-                copy_of(phase, way).wait_send()
+    def wait_sent():
+        for way, whole in (
+            (RIGHT, ext_w0.at[pl.ds(0, 4 * reach)]), (LEFT, ext_w0.at[pl.ds(0, 4 * reach)]),
+            (DOWN, pack.at[0]), (UP, pack.at[1]),
+        ):
+            @pl.when(has[way])
+            def _():
+                remote(whole, whole, 0, way, way, target[way]).wait_send()
         if relayed:
-            @pl.when(jnp.logical_or(rad == 0, rad == 3))
-            def _():
-                remote(relay.at[phase], above.at[phase, high], phase, FORWARD, DOWN_HI, across).wait_send()
+            @pl.when(ends)
+            def _():
+                remote(relay, relay, 0, FORWARD, DOWN_HI, across).wait_send()
 
     row = lax.broadcasted_iota(jnp.int32, (nrows, ncols), 0)
     col = lax.broadcasted_iota(jnp.int32, (nrows, ncols), 1)
@@ -196,7 +199,7 @@
                 tile = None
                 for k in range(group):
                     tile = packed(ext[reach + q * group + k], side, k, tile)
-                pack[phase, side, q] = tile
+                pack[side, phase, q] = tile
             return carry
 
         lax.fori_loop(0, nchan // group, step, 0)
@@ -234,7 +237,7 @@
 
         lax.fori_loop(0, nchan, step, 0, unroll=group * 2)
 
-    def edge_part(phase, base, emit, packs=None):
+    def edge_part(phase, part, base, emit, packs=None):
         def step(q, carry):
             upper, lower = above[phase, q], below[phase, q]
             tiles = [None, None]
@@ -247,17 +250,37 @@
                     tiles = [packed(value, side, k, tiles[side]) for side in range(2)]
             if packs is not None:
                 for side in range(2):
-                    pack[packs, side, q] = tiles[side]
+                    pack[side, packs, q] = tiles[side]
             return carry
 
-        lax.fori_loop(0, nchan // group, step, 0)
+        lax.fori_loop(*halves[part], step, 0)
 
     fills[0].wait()
     pack_rows(0)
-    neighbours = sum(has[way].astype(jnp.int32) for way in range(4)) + int(relayed)
-    pl.semaphore_wait(barrier, neighbours)
-    send_rows(0)
-    send_channels(0)
+    partners = sum(meets[way].astype(jnp.int32) for way in range(4)) + int(relayed)
+    pl.semaphore_wait(barrier, partners)
+    if relayed:
+        for here, there in ((0, 1), (3, 2)):
+            @pl.when(rad == here)
+            def _():
+                pl.semaphore_signal(
+                    met_sem, inc=1, device_id={"rad": there}, device_id_type=pl.DeviceIdType.MESH
+                )
+    send_far(0, 1)
+    send_near(0, 0)
+    send_near(0, 1)
+    send_channel(0, RIGHT)
+    send_channel(0, LEFT)
+    fills[1].wait()
+    pack_rows(1)
+    if relayed:
+        @pl.when(mids)
+        def _():
+            pl.semaphore_wait(met_sem, 1)
+    send_far(0, 0)
+    send_far(1, 0)
+    send_far(1, 1)
+    send_near(1, 0)
     for copy in tables:
         copy.wait()
 
@@ -277,40 +300,43 @@
     def emit_out1(c, total):
         out_ref[1, c] = ext_w1[reach + c] + ext_f1[reach + c] - (0.5 * time_step) * total
 
+    def advance(phase, base, emit):
+        for part in range(2):
+            receive_rows(phase, part)
+            edge_part(phase, part, base, emit, phase + 2)
+            send_far(phase + 2, part)
+            send_near(phase + 2, part)
+            send_channel(phase + 2, (LEFT, RIGHT)[part])
+
+    def finish(phase, base, emit):
+        for part in range(2):
+            receive_rows(phase, part)
+            edge_part(phase, part, base, emit)
+
     local_part(0, base_a)
-    fills[1].wait()
-    pack_rows(1)
+    forward(0)
+    send_near(1, 1)
+    send_channel(1, RIGHT)
+    send_channel(1, LEFT)
     local_part(1, base_b)
-    forward(0)
-    send_rows(1)
-    send_channels(1)
+    forward(1)
     receive_channels(0)
     coupled_part(0, base_a)
-    forward(1)
-    receive_rows(0)
-    edge_part(0, base_a, emit_f1, 2)
-    send_rows(2)
-    send_channels(2)
+    advance(0, base_a, emit_f1)
     local_part(2, base_a)
     receive_channels(1)
     coupled_part(1, base_b)
+    advance(1, base_b, emit_f0)
     forward(2)
-    receive_rows(1)
-    edge_part(1, base_b, emit_f0, 3)
-    send_rows(3)
-    send_channels(3)
     local_part(3, base_b)
     receive_channels(2)
     coupled_part(2, base_a)
     forward(3)
-    receive_rows(2)
-    edge_part(2, base_a, emit_out0)
     receive_channels(3)
     coupled_part(3, base_b)
-    receive_rows(3)
-    edge_part(3, base_b, emit_out1)
-    for phase in range(4):
-        wait_sent(phase)
+    finish(2, base_a, emit_out0)
+    finish(3, base_b, emit_out1)
+    wait_sent()
 
 
 def body(wave_field, partner, coupling_kind, coupling, angular):
@@ -331,14 +357,15 @@
             *(pltpu.SMEM(table.shape, table.dtype) for table in tables),
             pltpu.VMEM((KINDS + 2, nrows, ncols), f32),
             ext, ext, ext, ext, base, base,
-            pltpu.VMEM((4, 2, tiles, nrows, ncols), f32),
+            pltpu.VMEM((2, 4, tiles, nrows, ncols), f32),
             pltpu.VMEM((4, tiles, nrows, ncols), f32),
             pltpu.VMEM((4, tiles, nrows, ncols), f32),
             pltpu.VMEM((4, tiles // 2, nrows, ncols), f32),
             pltpu.SemaphoreType.DMA((4,)),
             pltpu.SemaphoreType.DMA((2,)),
-            pltpu.SemaphoreType.DMA((4, 8)),
-            pltpu.SemaphoreType.DMA((4, 8)),
+            pltpu.SemaphoreType.DMA((5,)),
+            pltpu.SemaphoreType.DMA((4, 6)),
+            pltpu.SemaphoreType.REGULAR,
         ],
         compiler_params=pltpu.CompilerParams(
             collective_id=0, has_side_effects=True, vmem_limit_bytes=67_043_328 - 4 * wave_field.size

time: 24.3 us -> 23.9 us (0.984)
  Pallas kernels: 23.2 us -> 22.8 us
    pallas_call x1, Pallas kernels: 23.2 us -> 22.8 us  [body(): pl.pallas_call(kernel, out_shape=pltpu.VMEM(wave_field.shape, f32), in_sp...]
where the time goes in v2:
time: 23.9 us; the launch traced here: 23.7 us
  Pallas kernels  22.8 us (95%)
  local copies, waits for them, and re-layouts  0.97 us (4%)
    pallas_call x1, Pallas kernels, body(): pl.pallas_call(kernel, out_shape=pltpu.VMEM(wave_field.shape, f32), in_sp...  22.8 us
    unnamed x1, local copies, waits for them, and re-layouts  0.97 us

profile of v2, /device:TPU:0, one launch (start us, length us, event | category | flops | bytes accessed | tf_op | source)
XLA Modules:
  0.0 23.7 jit_solution(1242055244941808381)
XLA Ops:
  0.0 22.8 %taylor_step.1 = f32[2,16,8,1024]{3,2,1,0:T(8,128)S(1)} custom-call(s32[8,128]{1,0:T(8,128)} %bitcast.4, s32[8,128]{1,0:T(8,128)} %bitcast.5, f32[8,128]{1,0:T(8,128)} %bitcast.6, s32[2,128]{1,0:T(2,128)} %bitcast.7, f32[2,16,8,1024]{3,2,1,0:T(8,128)} %wave_ref.1), custom_call_target="tpu_custom_call" | custom-call | tf_op jit(solution)/shard_map/taylor_step/pallas_call | solution.py:351
  22.8 1.0 %copy.7 = f32[2,16,8,1024]{3,2,1,0:T(8,128)} copy(f32[2,16,8,1024]{3,2,1,0:T(8,128)S(1)} %taylor_step.1) | data formatting | bytes 2097152
